TPU v7x, 32 devices: a whole 2x2x4 slice. The times are simulated.
32 devices in a mesh: occ: 8 (over z, x), vir: 4 (over y, core).
Axes of the slice: x: 2, y: 2, z: 4, core: 2. Of those that a mesh axis runs over, the one named last changes fastest.
Arguments:
- b_occ: bfloat16 [32, 768, 2304], P('occ', 'vir'), may hold values from -0.86328125 to 0.86328125
- b_outer: bfloat16 [2, 768, 2304], P(None, 'vir', 'occ'), may hold values from -0.86328125 to 0.86328125
- eps_occ: float32 [32], P('occ'), may hold values from -1.5 to -0.3
- eps_outer: float32 [2], replicated, may hold values from -1.5 to -0.3
- eps_vir: float32 [768], P('vir'), may hold values from 0.2 to 3
Outputs:
- gamma_occ: float32 [32, 768, 2304], P('occ', 'vir')
- gamma_outer: float32 [2, 768, 2304], P(None, 'vir', 'occ')
All inputs are finite; a program needn't handle non-finite values.
Results may differ from a plain program's by a relative error of at most 0.0018.
Values may be sent and summed in bfloat16 or wider, within the bound.
A program may use at most 128 MiB of HBM per device.

v0:
```python
import functools

import jax
import jax.numpy as jnp
from jax import lax
from jax.experimental import pallas as pl
from jax.experimental.pallas import tpu as pltpu
from jax.sharding import PartitionSpec as P

MESH = pl.DeviceIdType.MESH
F32 = jnp.float32
BF16 = jnp.bfloat16
VMEM_SPEC = pl.BlockSpec(memory_space=pltpu.VMEM)
SMEM_SPEC = pl.BlockSpec(memory_space=pltpu.SMEM)
ANY_SPEC = pl.BlockSpec(memory_space=pl.ANY)
LIMIT = 60 * 1024 * 1024


def encode(x):
    square = x * x
    fourth = square * square
    return jnp.where(x < 0, -fourth, fourth).astype(BF16)


def decode(code):
    y = code.astype(F32)
    root = lax.rsqrt(lax.rsqrt(jnp.abs(y)))
    return jnp.where(y < 0, -root, root)


class Place:
    def __init__(self, n_g, n_u):
        o, v = lax.axis_index("occ"), lax.axis_index("vir")
        self.n_g, self.n_u = n_g, n_u
        self.o, self.v = o, v
        self.g, self.r = o // 2, o % 2
        self.u, self.c = v // 2, v % 2

    def up_g(self, s):
        return (self.g + s) % self.n_g

    def down_g(self, s):
        return (self.g + self.n_g - s) % self.n_g

    def up_u(self, t):
        return (self.u + t) % self.n_u

    def down_u(self, t):
        return (self.u + self.n_u - t) % self.n_u

    def x_peer(self):
        return (self.g * 2 + 1 - self.r, self.v)

    def c_peer(self):
        return (self.o, self.u * 2 + 1 - self.c)

    def y_peer(self, t):
        return (self.o, self.up_u(t) * 2 + self.c)

    def z_peer(self, s):
        return (self.up_g(s) * 2 + self.r, self.v)

    def greet(self, peers):
        barrier = pltpu.get_barrier_semaphore()
        for peer in peers:
            pl.semaphore_signal(barrier, inc=1, device_id=peer, device_id_type=MESH)
        pl.semaphore_wait(barrier, len(peers))


def remote(src, dst, send_sem, recv_sem, peer):
    return pltpu.make_async_remote_copy(
        src_ref=src, dst_ref=dst, send_sem=send_sem, recv_sem=recv_sem, device_id=peer, device_id_type=MESH
    )


def gather_kernel(n_g, n_u, own, eps, b_occ, out, eps_out, b_turned, b_in, b_out, local_sem, send, z_sem, x_sem, y_sem, d_sem, c_sem, e_send, e_sem):
    me = Place(n_g, n_u)
    n_vir = 2 * n_u
    fetch = pltpu.make_async_copy(b_occ, b_in, local_sem.at[2])
    fetch.start()
    vir_peers = [(me.o, (me.v + k) % n_vir) for k in range(1, n_vir)]
    me.greet([me.z_peer(s) for s in range(1, n_g)] + [me.x_peer()] + vir_peers)
    started = []

    def slot(g, r, u, c):
        return out.at[u * 2 + c, g * 2 + r]

    def go(src, place, recv_sem, peer):
        copy = remote(src, place, send.at[len(started)], recv_sem, peer)
        copy.start()
        started.append(copy)

    def arrived(place, sem):
        remote(place, place, send.at[0], sem, me.x_peer()).wait_recv()

    mine = slot(me.g, me.r, me.u, me.c)
    for s in range(1, n_g):
        go(own, mine, z_sem.at[s - 1], me.z_peer(s))
    go(own, mine, x_sem.at[0], me.x_peer())
    for t in range(1, n_u):
        go(own, mine, y_sem.at[0, t - 1], me.y_peer(t))
    go(own, mine, c_sem.at[0, 0, 0], me.c_peer())
    local = pltpu.make_async_copy(own, mine, local_sem.at[0])
    local.start()
    eps_local = pltpu.make_async_copy(eps, eps_out.at[me.v], local_sem.at[1])
    eps_local.start()
    eps_copies = [
        remote(eps, eps_out.at[me.v], e_send.at[k], e_sem.at[k], peer) for k, peer in enumerate(vir_peers)
    ]
    for copy in eps_copies:
        copy.start()

    def relay_z(s):
        place = slot(me.down_g(s), me.r, me.u, me.c)
        arrived(place, z_sem.at[s - 1])
        go(place, place, x_sem.at[s], me.x_peer())
        for t in range(1, n_u):
            go(place, place, y_sem.at[s, t - 1], me.y_peer(t))
        go(place, place, c_sem.at[s, 0, 0], me.c_peer())

    def relay_xy(s):
        place = slot(me.down_g(s), 1 - me.r, me.u, me.c)
        arrived(place, x_sem.at[s])
        if s % 2 == 0:
            for t in range(1, n_u):
                go(place, place, d_sem.at[s, t - 1], me.y_peer(t))
        go(place, place, c_sem.at[s, 1, 0], me.c_peer())
        for t in range(1, n_u):
            place = slot(me.down_g(s), me.r, me.down_u(t), me.c)
            arrived(place, y_sem.at[s, t - 1])
            if s % 2 == 1:
                go(place, place, d_sem.at[s, t - 1], me.x_peer())
            go(place, place, c_sem.at[s, 0, t], me.c_peer())

    depth = b_in.shape[1]
    tile = next(k for k in (256, 128) if depth % k == 0)

    def turn(k, carry):
        at = pl.ds(pl.multiple_of(k * tile, tile), tile)
        b_out[at, :] = b_in[:, at].T
        return carry

    tiles = depth // tile
    edges = [tiles * k // n_g for k in range(n_g + 1)]
    for s in range(n_g):
        if s + 1 < n_g:
            relay_z(s + 1)
        if s == 0:
            fetch.wait()
        relay_xy(s)
        lax.fori_loop(edges[s], edges[s + 1], turn, 0)
    store = pltpu.make_async_copy(b_out, b_turned, local_sem.at[2])
    store.start()
    for s in range(n_g):
        for t in range(1, n_u):
            place = slot(me.down_g(s), 1 - me.r, me.down_u(t), me.c)
            arrived(place, d_sem.at[s, t - 1])
            go(place, place, c_sem.at[s, 1, t], me.c_peer())
    for s in range(n_g):
        for q in range(2):
            for t in range(n_u):
                r = me.r if q == 0 else 1 - me.r
                arrived(slot(me.down_g(s), r, me.down_u(t), 1 - me.c), c_sem.at[s, q, t])
    local.wait()
    eps_local.wait()
    store.wait()
    for k, copy in enumerate(eps_copies):
        copy.wait_send()
        source = (me.v + n_vir - 1 - k) % n_vir
        remote(eps, eps_out.at[source], e_send.at[k], e_sem.at[k], vir_peers[k]).wait_recv()
    for copy in started:
        copy.wait_send()


def gather(own, eps, b_occ, n_g, n_u):
    qs, w = own.shape
    n_vir = 2 * n_u
    dma = pltpu.SemaphoreType.DMA
    messages = (n_g - 1) + n_g + 2 * n_g * (n_u - 1) + 2 * n_g * n_u
    return pl.pallas_call(
        functools.partial(gather_kernel, n_g, n_u),
        out_shape=(
            jax.ShapeDtypeStruct((n_vir, 2 * n_g, qs, w), own.dtype),
            jax.ShapeDtypeStruct((n_vir,) + eps.shape, eps.dtype),
            jax.ShapeDtypeStruct(b_occ.shape[::-1], b_occ.dtype),
        ),
        in_specs=[VMEM_SPEC, VMEM_SPEC, ANY_SPEC],
        out_specs=(ANY_SPEC, VMEM_SPEC, ANY_SPEC),
        scratch_shapes=[
            pltpu.VMEM(b_occ.shape, b_occ.dtype),
            pltpu.VMEM(b_occ.shape[::-1], b_occ.dtype),
            dma((3,)),
            dma((messages,)),
            dma((n_g,)),
            dma((n_g,)),
            dma((n_g, max(n_u - 1, 1))),
            dma((n_g, max(n_u - 1, 1))),
            dma((n_g, 2, n_u)),
            dma((n_vir - 1,)),
            dma((n_vir - 1,)),
        ],
        compiler_params=pltpu.CompilerParams(collective_id=0, has_side_effects=True, vmem_limit_bytes=LIMIT),
    )(own, eps, b_occ)


def amplitude_kernel(
    n_vir, n_i, n_j, b_occ, b_whole, e_occ, e_outer, e_mine, e_all,
    hi, lo, amps, sent, got, blocks, b_sem, send_sem, recv_sem,
):
    o, v = lax.axis_index("occ"), lax.axis_index("vir")
    u, c, n_u = v // 2, v % 2, n_vir // 2
    steps = [(t, e) for t in range(1, n_u) for e in range(2)] + [(0, 1), (0, 0)]
    far = n_vir - 1
    targets = [(u + t) % n_u * 2 + (c + e) % 2 for t, e in steps]
    sources = [(u + n_u - t) % n_u * 2 + (c + e) % 2 for t, e in steps]
    rows = b_occ.shape[0]
    vl = rows // n_i

    def load(k):
        return pltpu.make_async_copy(b_whole.at[targets[k]], blocks.at[k % 2], b_sem.at[k % 2])

    load(0).start()
    barrier = pltpu.get_barrier_semaphore()
    for peer in targets[:far]:
        pl.semaphore_signal(barrier, inc=1, device_id=(o, peer), device_id_type=MESH)
    pl.semaphore_wait(barrier, far)

    row = e_mine[...].T[:, 0:1]
    copies = []
    for k, target in enumerate(targets):
        if k + 1 < n_vir:
            load(k + 1).start()
        load(k).wait()
        amps[target] = jnp.dot(b_occ[...], blocks[k % 2], preferred_element_type=F32)
        col = jnp.concatenate([e_outer[j] - e_all[target, 0:1, :] for j in range(n_j)], axis=1)

        def part(i, carry, k=k, target=target, col=col):
            at = pl.ds(pl.multiple_of(i * vl, vl), vl)
            value = amps[target, at, :] / ((e_occ[i] - row) + col)
            amps[target, at, :] = value
            code = encode(value)
            if k < far:
                sent[k, at, :] = code
            else:
                got[target, at, :] = code
            return carry

        lax.fori_loop(0, n_i, part, 0)
        if k < far:
            copy = remote(sent.at[k], got.at[v], send_sem.at[k], recv_sem.at[k], (o, target))
            copy.start()
            copies.append(copy)

    def finish(source):
        def part(i, carry):
            at = pl.ds(pl.multiple_of(i * vl, vl), vl)
            turned = decode(got[source, at, :]).T
            swapped = jnp.concatenate([turned[j * vl : (j + 1) * vl] for j in range(n_j)], axis=1)
            tilde = 2.0 * amps[source, at, :] - swapped
            high = tilde.astype(BF16)
            hi[source, at, :] = high
            lo[source, at, :] = (tilde - high.astype(F32)).astype(BF16)
            return carry

        lax.fori_loop(0, n_i, part, 0)

    finish(v)
    for k in [far - 1] + list(range(far - 1)):
        source = sources[k]
        remote(sent.at[k], got.at[source], send_sem.at[k], recv_sem.at[k], (o, source)).wait_recv()
        finish(source)
    for copy in copies:
        copy.wait_send()


def amplitudes(b_occ, b_whole, e_occ, e_outer, e_mine, e_all):
    n_i, n_j = e_occ.shape[0], e_outer.shape[0]
    n_vir, _, w = b_whole.shape
    rows = b_occ.shape[0]
    dma = pltpu.SemaphoreType.DMA
    shape = jax.ShapeDtypeStruct((n_vir, rows, w), BF16)
    return pl.pallas_call(
        functools.partial(amplitude_kernel, n_vir, n_i, n_j),
        out_shape=(shape, shape),
        in_specs=[VMEM_SPEC, ANY_SPEC, SMEM_SPEC, SMEM_SPEC, VMEM_SPEC, VMEM_SPEC],
        out_specs=(VMEM_SPEC, VMEM_SPEC),
        scratch_shapes=[
            pltpu.VMEM((n_vir, rows, w), F32),
            pltpu.VMEM((n_vir - 1, rows, w), BF16),
            pltpu.VMEM((n_vir, rows, w), BF16),
            pltpu.VMEM((2,) + b_whole.shape[1:], BF16),
            dma((2,)),
            dma((n_vir - 1,)),
            dma((n_vir - 1,)),
        ],
        compiler_params=pltpu.CompilerParams(collective_id=1, has_side_effects=True, vmem_limit_bytes=LIMIT),
    )(b_occ, b_whole, e_occ, e_outer, e_mine, e_all)


def reduce_kernel(
    n_g, n_u, chunk, b_turned, b_whole, hi, lo, gamma, result,
    b_local, held, sums, c_out, c_in, out, d_in, x_in, y_in, z_in,
    b_sem, g_sem, c_send, c_sem, send, d_sem, x_sem, y_sem, z_sem,
):
    me = Place(n_g, n_u)
    n_vir = 2 * n_u
    qs = c_out.shape[2]
    depth = b_whole.shape[1]
    fetch = pltpu.make_async_copy(b_whole, b_local, b_sem)
    fetch.start()
    me.greet(
        [me.z_peer(s) for s in range(1, n_g)]
        + [me.x_peer(), me.c_peer()]
        + [me.y_peer(t) for t in range(1, n_u)]
    )
    started = []

    def product(s, t, c, store):
        g = (me.g + s) % n_g
        v = (me.u + t) % n_u * 2 + c
        at = pl.ds(pl.multiple_of(g * 2 * qs, 2 * qs), 2 * qs)
        both = jnp.dot(
            b_turned[at, :], jnp.concatenate([hi[v], lo[v]], axis=1), preferred_element_type=F32
        )
        width = hi.shape[2]
        both = both[:, :width] + both[:, width:]
        store(me.r * n_u + t, both[:qs])
        store((1 - me.r) * n_u + t, both[qs:])

    def go(src, dst, send_sem, recv_sem, peer):
        copy = remote(src, dst, send_sem, recv_sem, peer)
        copy.start()
        started.append(copy)

    def arrived(dst, sem):
        remote(dst, dst, sem, sem, me.x_peer()).wait_recv()

    def ship(s, q, dst, sem, peer):
        out[s, q] = encode(sums[s, q])
        go(out.at[s, q], dst, send.at[s, q], sem, peer)

    def take(s, q, src, sem):
        arrived(src, sem)
        sums[s, q] = sums[s, q] + decode(src[...])

    done = [0]

    def out_copy(k):
        slot = k % 2
        at = pl.ds(pl.multiple_of(k * chunk, chunk), chunk)
        return pltpu.make_async_copy(held.at[slot], gamma.at[:, at], g_sem.at[slot])

    def fill(count):
        def part(k, carry):
            @pl.when(k >= 2)
            def _():
                out_copy(k - 2).wait()

            at = pl.ds(pl.multiple_of(k * chunk, chunk), chunk)
            right = jnp.concatenate([b_local[v, at, :] for v in range(n_vir)], axis=1)
            total = None
            for part_of in (hi, lo):
                left = jnp.concatenate([part_of[v] for v in range(n_vir)], axis=1)
                term = lax.dot_general(left, right, (((1,), (1,)), ((), ())), preferred_element_type=F32)
                total = term if total is None else total + term
            held[k % 2] = total
            out_copy(k).start()
            return carry

        if done[0] == 0:
            fetch.wait()
        last = min(done[0] + count, depth // chunk)
        if last > done[0]:
            lax.fori_loop(done[0], last, part, 0)
        done[0] = last

    share = max(depth // chunk // 4, 1)
    turn = [s % n_g for s in range(1, n_g + 1)]

    def first(s):
        def keep(q, value):
            sums[s, q] = value

        def code(q, value):
            c_out[s, q] = encode(value)

        def theirs(t, carry):
            product(s, t, 1 - me.c, code)
            return carry

        def ours(t, carry):
            product(s, t, me.c, keep)
            return carry

        lax.fori_loop(0, n_u, theirs, 0)
        for q in range(2 * n_u):
            go(c_out.at[s, q], c_in.at[s, q], c_send.at[s, q], c_sem.at[s, q], me.c_peer())
        lax.fori_loop(0, n_u, ours, 0)
        for q in reversed(range(2 * n_u)):
            take(s, q, c_in.at[s, q], c_sem.at[s, q])
            t = q - n_u
            if t > 0:
                peer = me.y_peer(t) if s % 2 == 0 else me.x_peer()
                ship(s, q, d_in.at[s, t - 1], d_sem.at[s, t - 1], peer)
        if s % 2 == 0:
            for t in range(1, n_u):
                ship(s, t, y_in.at[s, t - 1], y_sem.at[s, t - 1], me.y_peer(t))
        else:
            ship(s, n_u, x_in.at[s], x_sem.at[s], me.x_peer())

    def second(s):
        for t in range(1, n_u):
            q = n_u if s % 2 == 0 else t
            take(s, q, d_in.at[s, t - 1], d_sem.at[s, t - 1])
        if s % 2 == 0:
            ship(s, n_u, x_in.at[s], x_sem.at[s], me.x_peer())
        else:
            for t in range(1, n_u):
                ship(s, t, y_in.at[s, t - 1], y_sem.at[s, t - 1], me.y_peer(t))

    def third(s):
        take(s, 0, x_in.at[s], x_sem.at[s])
        for t in range(1, n_u):
            take(s, 0, y_in.at[s, t - 1], y_sem.at[s, t - 1])
        if s:
            ship(s, 0, z_in.at[s - 1], z_sem.at[s - 1], me.z_peer(s))

    first(turn[0])
    first(turn[1])
    for k in range(n_g + 1):
        if k < n_g:
            second(turn[k])
        if k + 2 < n_g:
            first(turn[k + 2])
        else:
            fill(share)
        if k >= 1:
            third(turn[k - 1])
    fill(depth // chunk)
    for s in range(1, n_g):
        take(0, 0, z_in.at[s - 1], z_sem.at[s - 1])
    result[...] = sums[0, 0]
    for k in range(max(depth // chunk - 2, 0), depth // chunk):
        out_copy(k).wait()
    for copy in started:
        copy.wait_send()


def reduce(b_turned, b_whole, hi, lo, n_g, n_u):
    depth, rows = b_turned.shape
    w = b_whole.shape[2]
    qs = depth // (2 * n_g)
    dma = pltpu.SemaphoreType.DMA
    chunk = next(k for k in (256, 128) if depth % k == 0)
    far = max(n_u - 1, 1)
    every = (n_g, 2 * n_u, qs, w)
    return pl.pallas_call(
        functools.partial(reduce_kernel, n_g, n_u, chunk),
        out_shape=(jax.ShapeDtypeStruct((rows, depth), F32), jax.ShapeDtypeStruct((qs, w), F32)),
        in_specs=[VMEM_SPEC, ANY_SPEC, VMEM_SPEC, VMEM_SPEC],
        out_specs=(ANY_SPEC, VMEM_SPEC),
        scratch_shapes=[
            pltpu.VMEM(b_whole.shape, b_whole.dtype),
            pltpu.VMEM((2, rows, chunk), F32),
            pltpu.VMEM(every, F32),
            pltpu.VMEM(every, BF16),
            pltpu.VMEM(every, BF16),
            pltpu.VMEM(every, BF16),
            pltpu.VMEM((n_g, far, qs, w), BF16),
            pltpu.VMEM((n_g, qs, w), BF16),
            pltpu.VMEM((n_g, far, qs, w), BF16),
            pltpu.VMEM((n_g, qs, w), BF16),
            dma,
            dma((2,)),
            dma(every[:2]),
            dma(every[:2]),
            dma(every[:2]),
            dma((n_g, far)),
            dma((n_g,)),
            dma((n_g, far)),
            dma((n_g,)),
        ],
        compiler_params=pltpu.CompilerParams(collective_id=2, has_side_effects=True, vmem_limit_bytes=LIMIT),
    )(b_turned, b_whole, hi, lo)


def on_device(n_occ, n_vir, b_occ, b_outer, eps_occ, eps_outer, eps_vir):
    n_g, n_u = n_occ // 2, n_vir // 2
    n_i, vl, depth = b_occ.shape
    n_j, _, qs = b_outer.shape
    own = b_outer.transpose(2, 0, 1).reshape(qs, n_j * vl)
    eps_rows = jnp.broadcast_to(eps_vir[None, :], (8, vl))
    flat = b_occ.reshape(n_i * vl, depth)
    b_whole, eps_all, b_turned = gather(own, eps_rows, flat, n_g, n_u)
    b_whole = b_whole.reshape(n_vir, depth, n_j * vl)
    hi, lo = amplitudes(flat, b_whole, eps_occ, eps_outer, eps_rows, eps_all)
    gamma_occ, mine = reduce(b_turned, b_whole, hi, lo, n_g, n_u)
    gamma_outer = mine.reshape(qs, n_j, vl).transpose(1, 2, 0)
    return gamma_occ.reshape(b_occ.shape), gamma_outer


def solution(mesh):
    placed = (P("occ", "vir", None), P(None, "vir", "occ"), P("occ"), P(), P("vir"))
    return jax.shard_map(
        functools.partial(on_device, mesh.shape["occ"], mesh.shape["vir"]),
        mesh=mesh,
        in_specs=placed,
        out_specs=(P("occ", "vir", None), P(None, "vir", "occ")),
        check_vma=False,
    )
```

profile of v0, /device:TPU:0, one launch (start us, length us, event | category | flops | bytes accessed | tf_op | source)
XLA Modules:
  0.0 154.4 jit_solution(11086117090332091744)
XLA Ops:
  0.6 1.3 broadcast_in_dim.2.eps.e_mine
  1.9 1.8 %copy.9.own = bf16[288,384]{1,0:T(8,128)(2,1)} copy(bf16[288,384]{0,1:T(8,128)(2,1)} %bitcast.15) | data formatting | bytes 442368 | tf_op jit(solution)/shard_map/reshape | solution.py:491
  3.7 45.7 %shard_map.68 = (bf16[4,8,288,384]{3,2,1,0:T(8,128)(2,1)}, f32[4,8,192]{2,1,0:T(8,128)}, bf16[2304,768]{1,0:T(8,128)(2,1)}) custom-call(bf16[288,384]{1,0:T(8,128)(2,1)} %copy.9.own, f32[8,192]{1,0:T(8,128)} %broadcast_in_dim.2.eps.e_mine, bf16[768,2304]{1,0:T(8,128)(2,1)} %bitcast.11), custom_call_target="tpu_custom_call" | custom-call | tf_op jit(solution)/shard_map/pallas_call | solution.py:180
  49.4 37.0 %shard_map.69 = (bf16[4,768,384]{2,1,0:T(8,128)(2,1)}, bf16[4,768,384]{2,1,0:T(8,128)(2,1)}) custom-call(bf16[768,2304]{1,0:T(8,128)(2,1)} %bitcast.12, bf16[4,2304,384]{2,1,0:T(8,128)(2,1)} %bitcast.9, f32[4]{0:T(128)} %e_occ.1, f32[2]{0:T(128)} %e_outer.1, f32[8,192]{1,0:T(8,128)} %broadcast_in_dim.2.eps.e_mine, f32[4,8,192]{2,1,0:T(8,128)} %get-tuple-element.11.e_all), custom_call_target="tpu_custom_call" | custom-call | tf_op jit(solution)/shard_map/pallas_call | solution.py:282
  86.4 59.5 %shard_map.70 = (f32[768,2304]{1,0:T(8,128)}, f32[288,384]{1,0:T(8,128)}) custom-call(bf16[2304,768]{1,0:T(8,128)(2,1)} %get-tuple-element.9.b_turned, bf16[4,2304,384]{2,1,0:T(8,128)(2,1)} %bitcast.10, bf16[4,768,384]{2,1,0:T(8,128)(2,1)} %get-tuple-element.12.hi, bf16[4,768,384]{2,1,0:T(8,128)(2,1)} %get-tuple-element.13.lo), custom_call_target="tpu_custom_call" | custom-call | tf_op jit(solution)/shard_map/pallas_call | solution.py:457
  145.9 2.1 %copy.10 = f32[288,384]{0,1:T(8,128)} copy(f32[288,384]{1,0:T(8,128)} %get-tuple-element.15) | data formatting | bytes 884736 | tf_op jit(solution)/shard_map/reshape | solution.py:498
  148.0 6.4 %copy.12 = f32[4,192,2304]{2,1,0:T(8,128)} copy(f32[4,192,2304]{2,1,0:T(8,128)} %bitcast.13) | data formatting | bytes 14155776
where the time goes:
time: 155 us; the launch traced here: 154 us
  Pallas kernels  142 us (92%)
  local copies, waits for them, and re-layouts  11.6 us (7%)
    pallas_call x1, Pallas kernels, reduce(): pl.pallas_call(functools.partial(reduce_kernel, n_g, n_u, chunk), out_sha...  59.5 us
    pallas_call x1, Pallas kernels, gather(): pl.pallas_call(functools.partial(gather_kernel, n_g, n_u), out_shape=(jax...  45.7 us
    pallas_call x1, Pallas kernels, amplitudes(): pl.pallas_call(functools.partial(amplitude_kernel, n_vir, n_i, n_j), out_...  37 us
    unnamed x1, local copies, waits for them, and re-layouts  6.42 us

commit v1 on v0

--- a/solution.py
+++ b/solution.py
@@ -13,7 +13,7 @@
 VMEM_SPEC = pl.BlockSpec(memory_space=pltpu.VMEM)
 SMEM_SPEC = pl.BlockSpec(memory_space=pltpu.SMEM)
 ANY_SPEC = pl.BlockSpec(memory_space=pl.ANY)
-LIMIT = 60 * 1024 * 1024
+LIMIT = 62 * 1024 * 1024
 
 
 def encode(x):
@@ -94,7 +94,8 @@
         remote(place, place, send.at[0], sem, me.x_peer()).wait_recv()
 
     mine = slot(me.g, me.r, me.u, me.c)
-    for s in range(1, n_g):
+    near = sorted(range(n_g), key=lambda s: (min(s, n_g - s), s))
+    for s in near[1:]:
         go(own, mine, z_sem.at[s - 1], me.z_peer(s))
     go(own, mine, x_sem.at[0], me.x_peer())
     for t in range(1, n_u):
@@ -142,16 +143,16 @@
 
     tiles = depth // tile
     edges = [tiles * k // n_g for k in range(n_g + 1)]
-    for s in range(n_g):
-        if s + 1 < n_g:
-            relay_z(s + 1)
-        if s == 0:
+    for k, s in enumerate(near):
+        if k + 1 < n_g:
+            relay_z(near[k + 1])
+        if k == 0:
             fetch.wait()
         relay_xy(s)
-        lax.fori_loop(edges[s], edges[s + 1], turn, 0)
+        lax.fori_loop(edges[k], edges[k + 1], turn, 0)
     store = pltpu.make_async_copy(b_out, b_turned, local_sem.at[2])
     store.start()
-    for s in range(n_g):
+    for s in near:
         for t in range(1, n_u):
             place = slot(me.down_g(s), 1 - me.r, me.down_u(t), me.c)
             arrived(place, d_sem.at[s, t - 1])
@@ -203,12 +204,14 @@
     )(own, eps, b_occ)
 
 
-def amplitude_kernel(
-    n_vir, n_i, n_j, b_occ, b_whole, e_occ, e_outer, e_mine, e_all,
-    hi, lo, amps, sent, got, blocks, b_sem, send_sem, recv_sem,
+def window_kernel(
+    n_g, n_u, n_i, n_j, chunk, b_occ, b_turned_all, b_whole, e_occ, e_outer, e_mine, e_all, gamma, result,
+    hi, lo, amps, sent, got, b_turned,
+    b_local, held, sums, c_out, c_in, out, d_in, x_in, y_in, z_in,
+    f_sem, send_sem, recv_sem, b_sem, g_sem, c_send, c_sem, send, d_sem, x_sem, y_sem, z_sem,
 ):
     o, v = lax.axis_index("occ"), lax.axis_index("vir")
-    u, c, n_u = v // 2, v % 2, n_vir // 2
+    u, c, n_vir = v // 2, v % 2, 2 * n_u
     steps = [(t, e) for t in range(1, n_u) for e in range(2)] + [(0, 1), (0, 0)]
     far = n_vir - 1
     targets = [(u + t) % n_u * 2 + (c + e) % 2 for t, e in steps]
@@ -217,24 +220,25 @@
     vl = rows // n_i
 
     def load(k):
-        return pltpu.make_async_copy(b_whole.at[targets[k]], blocks.at[k % 2], b_sem.at[k % 2])
-
-    load(0).start()
-    barrier = pltpu.get_barrier_semaphore()
-    for peer in targets[:far]:
-        pl.semaphore_signal(barrier, inc=1, device_id=(o, peer), device_id_type=MESH)
-    pl.semaphore_wait(barrier, far)
+        return pltpu.make_async_copy(b_whole.at[targets[k]], b_local.at[targets[k]], b_sem.at[k])
+
+    for k in range(n_vir):
+        load(k).start()
+    fetch = pltpu.make_async_copy(b_turned_all, b_turned, f_sem)
+    fetch.start()
+    me = Place(n_g, n_u)
+    me.greet(
+        [(o, peer) for peer in targets[:far]] + [me.z_peer(s) for s in range(1, n_g)] + [me.x_peer()]
+    )
 
     row = e_mine[...].T[:, 0:1]
     copies = []
     for k, target in enumerate(targets):
-        if k + 1 < n_vir:
-            load(k + 1).start()
         load(k).wait()
-        amps[target] = jnp.dot(b_occ[...], blocks[k % 2], preferred_element_type=F32)
+        amps[target] = jnp.dot(b_occ[...], b_local[target], preferred_element_type=F32)
         col = jnp.concatenate([e_outer[j] - e_all[target, 0:1, :] for j in range(n_j)], axis=1)
 
-        def part(i, carry, k=k, target=target, col=col):
+        def divide(i, carry, k=k, target=target, col=col):
             at = pl.ds(pl.multiple_of(i * vl, vl), vl)
             value = amps[target, at, :] / ((e_occ[i] - row) + col)
             amps[target, at, :] = value
@@ -245,7 +249,7 @@
                 got[target, at, :] = code
             return carry
 
-        lax.fori_loop(0, n_i, part, 0)
+        lax.fori_loop(0, n_i, divide, 0)
         if k < far:
             copy = remote(sent.at[k], got.at[v], send_sem.at[k], recv_sem.at[k], (o, target))
             copy.start()
@@ -264,55 +268,16 @@
 
         lax.fori_loop(0, n_i, part, 0)
 
-    finish(v)
-    for k in [far - 1] + list(range(far - 1)):
+    def collect(k):
         source = sources[k]
         remote(sent.at[k], got.at[source], send_sem.at[k], recv_sem.at[k], (o, source)).wait_recv()
         finish(source)
-    for copy in copies:
-        copy.wait_send()
-
-
-def amplitudes(b_occ, b_whole, e_occ, e_outer, e_mine, e_all):
-    n_i, n_j = e_occ.shape[0], e_outer.shape[0]
-    n_vir, _, w = b_whole.shape
-    rows = b_occ.shape[0]
-    dma = pltpu.SemaphoreType.DMA
-    shape = jax.ShapeDtypeStruct((n_vir, rows, w), BF16)
-    return pl.pallas_call(
-        functools.partial(amplitude_kernel, n_vir, n_i, n_j),
-        out_shape=(shape, shape),
-        in_specs=[VMEM_SPEC, ANY_SPEC, SMEM_SPEC, SMEM_SPEC, VMEM_SPEC, VMEM_SPEC],
-        out_specs=(VMEM_SPEC, VMEM_SPEC),
-        scratch_shapes=[
-            pltpu.VMEM((n_vir, rows, w), F32),
-            pltpu.VMEM((n_vir - 1, rows, w), BF16),
-            pltpu.VMEM((n_vir, rows, w), BF16),
-            pltpu.VMEM((2,) + b_whole.shape[1:], BF16),
-            dma((2,)),
-            dma((n_vir - 1,)),
-            dma((n_vir - 1,)),
-        ],
-        compiler_params=pltpu.CompilerParams(collective_id=1, has_side_effects=True, vmem_limit_bytes=LIMIT),
-    )(b_occ, b_whole, e_occ, e_outer, e_mine, e_all)
-
-
-def reduce_kernel(
-    n_g, n_u, chunk, b_turned, b_whole, hi, lo, gamma, result,
-    b_local, held, sums, c_out, c_in, out, d_in, x_in, y_in, z_in,
-    b_sem, g_sem, c_send, c_sem, send, d_sem, x_sem, y_sem, z_sem,
-):
-    me = Place(n_g, n_u)
-    n_vir = 2 * n_u
+
+    finish(v)
+    collect(far - 1)
+    fetch.wait()
     qs = c_out.shape[2]
     depth = b_whole.shape[1]
-    fetch = pltpu.make_async_copy(b_whole, b_local, b_sem)
-    fetch.start()
-    me.greet(
-        [me.z_peer(s) for s in range(1, n_g)]
-        + [me.x_peer(), me.c_peer()]
-        + [me.y_peer(t) for t in range(1, n_u)]
-    )
     started = []
 
     def product(s, t, c, store):
@@ -367,8 +332,6 @@
             out_copy(k).start()
             return carry
 
-        if done[0] == 0:
-            fetch.wait()
         last = min(done[0] + count, depth // chunk)
         if last > done[0]:
             lax.fori_loop(done[0], last, part, 0)
@@ -377,7 +340,7 @@
     share = max(depth // chunk // 4, 1)
     turn = [s % n_g for s in range(1, n_g + 1)]
 
-    def first(s):
+    def multiply(s, first_t, last_t):
         def keep(q, value):
             sums[s, q] = value
 
@@ -392,10 +355,14 @@
             product(s, t, me.c, keep)
             return carry
 
-        lax.fori_loop(0, n_u, theirs, 0)
-        for q in range(2 * n_u):
-            go(c_out.at[s, q], c_in.at[s, q], c_send.at[s, q], c_sem.at[s, q], me.c_peer())
-        lax.fori_loop(0, n_u, ours, 0)
+        lax.fori_loop(first_t, last_t, theirs, 0)
+        for t in range(first_t, last_t):
+            for q in (t, n_u + t):
+                go(c_out.at[s, q], c_in.at[s, q], c_send.at[s, q], c_sem.at[s, q], me.c_peer())
+        lax.fori_loop(first_t, last_t, ours, 0)
+
+    def first(s):
+        multiply(s, 1, n_u)
         for q in reversed(range(2 * n_u)):
             take(s, q, c_in.at[s, q], c_sem.at[s, q])
             t = q - n_u
@@ -425,6 +392,10 @@
         if s:
             ship(s, 0, z_in.at[s - 1], z_sem.at[s - 1], me.z_peer(s))
 
+    for s in turn:
+        multiply(s, 0, 1)
+    for k in range(far - 1):
+        collect(k)
     first(turn[0])
     first(turn[1])
     for k in range(n_g + 1):
@@ -442,11 +413,12 @@
     result[...] = sums[0, 0]
     for k in range(max(depth // chunk - 2, 0), depth // chunk):
         out_copy(k).wait()
-    for copy in started:
+    for copy in started + copies:
         copy.wait_send()
 
 
-def reduce(b_turned, b_whole, hi, lo, n_g, n_u):
+def window(b_occ, b_turned, b_whole, e_occ, e_outer, e_mine, e_all, n_g, n_u):
+    n_vir, n_i, n_j = 2 * n_u, e_occ.shape[0], e_outer.shape[0]
     depth, rows = b_turned.shape
     w = b_whole.shape[2]
     qs = depth // (2 * n_g)
@@ -455,11 +427,17 @@
     far = max(n_u - 1, 1)
     every = (n_g, 2 * n_u, qs, w)
     return pl.pallas_call(
-        functools.partial(reduce_kernel, n_g, n_u, chunk),
+        functools.partial(window_kernel, n_g, n_u, n_i, n_j, chunk),
         out_shape=(jax.ShapeDtypeStruct((rows, depth), F32), jax.ShapeDtypeStruct((qs, w), F32)),
-        in_specs=[VMEM_SPEC, ANY_SPEC, VMEM_SPEC, VMEM_SPEC],
+        in_specs=[VMEM_SPEC, ANY_SPEC, ANY_SPEC, SMEM_SPEC, SMEM_SPEC, VMEM_SPEC, VMEM_SPEC],
         out_specs=(ANY_SPEC, VMEM_SPEC),
         scratch_shapes=[
+            pltpu.VMEM((n_vir, rows, w), BF16),
+            pltpu.VMEM((n_vir, rows, w), BF16),
+            pltpu.VMEM((n_vir, rows, w), F32),
+            pltpu.VMEM((n_vir - 1, rows, w), BF16),
+            pltpu.VMEM((n_vir, rows, w), BF16),
+            pltpu.VMEM(b_turned.shape, BF16),
             pltpu.VMEM(b_whole.shape, b_whole.dtype),
             pltpu.VMEM((2, rows, chunk), F32),
             pltpu.VMEM(every, F32),
@@ -471,6 +449,9 @@
             pltpu.VMEM((n_g, far, qs, w), BF16),
             pltpu.VMEM((n_g, qs, w), BF16),
             dma,
+            dma((n_vir - 1,)),
+            dma((n_vir - 1,)),
+            dma((n_vir,)),
             dma((2,)),
             dma(every[:2]),
             dma(every[:2]),
@@ -480,8 +461,8 @@
             dma((n_g, far)),
             dma((n_g,)),
         ],
-        compiler_params=pltpu.CompilerParams(collective_id=2, has_side_effects=True, vmem_limit_bytes=LIMIT),
-    )(b_turned, b_whole, hi, lo)
+        compiler_params=pltpu.CompilerParams(collective_id=1, has_side_effects=True, vmem_limit_bytes=LIMIT),
+    )(b_occ, b_turned, b_whole, e_occ, e_outer, e_mine, e_all)
 
 
 def on_device(n_occ, n_vir, b_occ, b_outer, eps_occ, eps_outer, eps_vir):
@@ -493,8 +474,7 @@
     flat = b_occ.reshape(n_i * vl, depth)
     b_whole, eps_all, b_turned = gather(own, eps_rows, flat, n_g, n_u)
     b_whole = b_whole.reshape(n_vir, depth, n_j * vl)
-    hi, lo = amplitudes(flat, b_whole, eps_occ, eps_outer, eps_rows, eps_all)
-    gamma_occ, mine = reduce(b_turned, b_whole, hi, lo, n_g, n_u)
+    gamma_occ, mine = window(flat, b_turned, b_whole, eps_occ, eps_outer, eps_rows, eps_all, n_g, n_u)
     gamma_outer = mine.reshape(qs, n_j, vl).transpose(1, 2, 0)
     return gamma_occ.reshape(b_occ.shape), gamma_outer
 

time: 155 us -> 142 us (0.916)
  Pallas kernels: 142 us -> 129 us
    pallas_call x2 -> x1, Pallas kernels: 96.5 us -> 86.2 us  [window(): pl.pallas_call(functools.partial(window_kernel, n_g, n_u, n_i, n_j, chunk...]
    pallas_call x1, Pallas kernels: 45.7 us -> 43.1 us  [gather(): pl.pallas_call(functools.partial(gather_kernel, n_g, n_u), out_shape=(jax...]
where the time goes in v1:
time: 142 us
  Pallas kernels  129 us (91%)
  local copies, waits for them, and re-layouts  11.6 us (8%)
    pallas_call x1, Pallas kernels, window(): pl.pallas_call(functools.partial(window_kernel, n_g, n_u, n_i, n_j, chunk...  86.2 us
    pallas_call x1, Pallas kernels, gather(): pl.pallas_call(functools.partial(gather_kernel, n_g, n_u), out_shape=(jax...  43.1 us
    unnamed x1, local copies, waits for them, and re-layouts  6.42 us

profile of v1, /device:TPU:0, one launch (start us, length us, event | category | flops | bytes accessed | tf_op | source)
XLA Modules:
  0.0 141.5 jit_solution(14635221767282026378)
XLA Ops:
  0.6 1.3 broadcast_in_dim.2.eps.e_mine
  1.9 1.8 %copy.9.own = bf16[288,384]{1,0:T(8,128)(2,1)} copy(bf16[288,384]{0,1:T(8,128)(2,1)} %bitcast.14) | data formatting | bytes 442368 | tf_op jit(solution)/shard_map/reshape | solution.py:472
  3.7 43.1 %shard_map.68 = (bf16[4,8,288,384]{3,2,1,0:T(8,128)(2,1)}, f32[4,8,192]{2,1,0:T(8,128)}, bf16[2304,768]{1,0:T(8,128)(2,1)}) custom-call(bf16[288,384]{1,0:T(8,128)(2,1)} %copy.9.own, f32[8,192]{1,0:T(8,128)} %broadcast_in_dim.2.eps.e_mine, bf16[768,2304]{1,0:T(8,128)(2,1)} %bitcast.9), custom_call_target="tpu_custom_call" | custom-call | tf_op jit(solution)/shard_map/pallas_call | solution.py:181
  46.8 86.2 %shard_map.69 = (f32[768,2304]{1,0:T(8,128)}, f32[288,384]{1,0:T(8,128)}) custom-call(bf16[768,2304]{1,0:T(8,128)(2,1)} %bitcast.10, bf16[2304,768]{1,0:T(8,128)(2,1)} %get-tuple-element.7.b_turned_all, bf16[4,2304,384]{2,1,0:T(8,128)(2,1)} %bitcast.11, f32[4]{0:T(128)} %e_occ.1, f32[2]{0:T(128)} %e_outer.1, f32[8,192]{1,0:T(8,128)} %broadcast_in_dim.2.eps.e_mine, ...), custom_call_target="tpu_custom_call" | custom-call | tf_op jit(solution)/shard_map/pallas_call | solution.py:429
  133.0 2.1 %copy.10 = f32[288,384]{0,1:T(8,128)} copy(f32[288,384]{1,0:T(8,128)} %get-tuple-element.11) | data formatting | bytes 884736 | tf_op jit(solution)/shard_map/reshape | solution.py:478
  135.1 6.4 %copy.12 = f32[4,192,2304]{2,1,0:T(8,128)} copy(f32[4,192,2304]{2,1,0:T(8,128)} %bitcast.12) | data formatting | bytes 14155776
